TPU v7x, 32 devices: a whole 2x2x4 slice. The times are simulated.
32 devices in a mesh: req: 8 (over z, x), tp: 4 (over y, core).
Axes of the slice: x: 2, y: 2, z: 4, core: 2. Of those that a mesh axis runs over, the one named last changes fastest.
Arguments:
- hidden: bfloat16 [512, 2048], P('req')
- norm_gain: float32 [2048], replicated, may hold values from 0.5 to 1.5
- head_weight: bfloat16 [2048, 12288], P(None, ('req', 'tp'))
- targets: int32 [512], P('req'), may hold values from 0 to 12287
- pad_mask: int32 [512], P('req'), may hold values 0 or 1
Outputs:
- logprob: float32 [512], P('req')
- entropy: float32 [512], P('req')
All inputs are finite; a program needn't handle non-finite values. No bound on the sum of `pad_mask` on one device may be relied on, other than what follows from the above.
Results may differ from a plain program's by a relative error of at most 0.0012.
Values may be sent and summed in bfloat16 or wider, within the bound.
A program may use at most 128 MiB of HBM per device.

v0:
```python
import jax
import jax.numpy as jnp
from jax import lax
from jax.sharding import PartitionSpec as P


def combined_all(value, axis, join):
    pieces = jax.tree.map(lambda part: lax.all_gather(part, axis), value)
    head = jax.tree.map(lambda part: part[0], pieces)
    tail = jax.tree.map(lambda part: part[1:], pieces)
    subtotal, _ = lax.scan(lambda subtotal, slab: (join(subtotal, slab), None), head, tail)
    return subtotal


def combine_stats(earlier, later):
    top_a, total_a, weighted_a, picked_a = earlier
    top_b, total_b, weighted_b, picked_b = later
    top_new = jnp.maximum(top_a, top_b)
    scale_a = jnp.exp(top_a - top_new)
    scale_b = jnp.exp(top_b - top_new)
    return (
        top_new,
        total_a * scale_a + total_b * scale_b,
        weighted_a * scale_a + weighted_b * scale_b,
        picked_a + picked_b,
    )


def body(hidden, norm_gain, head_weight, targets, pad_mask):
    slots = hidden.shape[0]
    voc_local = head_weight.shape[1]
    tp_count = lax.axis_size("tp")
    voc_start = (lax.axis_index("req") * tp_count + lax.axis_index("tp")) * voc_local
    wide = hidden.astype(jnp.float32)
    scale = lax.rsqrt(jnp.mean(wide * wide, axis=1, keepdims=True) + 1e-05)
    normed = (wide * scale * norm_gain[None, :]).astype(jnp.bfloat16)
    columns = lax.broadcasted_iota(jnp.int32, (1, voc_local), 1)
    all_targets = lax.all_gather(targets, "req", axis=0, tiled=True)
    logits = jnp.dot(
        lax.all_gather(normed, "req", axis=0, tiled=True),
        head_weight,
        preferred_element_type=jnp.float32,
    )
    top_row = jnp.max(logits, axis=1)
    expo = jnp.exp(logits - top_row[:, None])
    local = all_targets - voc_start
    picked_row = jnp.sum(jnp.where(columns == local[:, None], logits, jnp.float32(0.0)), axis=1)
    parts = (top_row, jnp.sum(expo, axis=1), jnp.sum(expo * logits, axis=1), picked_row)
    stats = tuple((fresh for fresh in parts))
    merged = combined_all(stats, ("req", "tp"), combine_stats)
    own_start = lax.axis_index("req") * slots
    top_all, total_all, weighted_all, picked_all = tuple(
        (lax.dynamic_slice_in_dim(whole, own_start, slots, 0) for whole in merged)
    )
    lse = top_all + jnp.log(total_all)
    live = pad_mask.astype(jnp.float32)
    logprob = (picked_all - lse) * live
    entropy = (lse - weighted_all / total_all) * live
    return (logprob, entropy)


def solution(mesh):
    return jax.shard_map(
        body,
        mesh=mesh,
        in_specs=(P("req", None), P(), P(None, ("req", "tp")), P("req"), P("req")),
        out_specs=(P("req"), P("req")),
        check_vma=False,
    )
```

profile of v0, /device:TPU:0, one launch (start us, length us, event | category | flops | bytes accessed | tf_op | source)
XLA Modules:
  0.0 227.5 jit_solution(6988182918797164582)
XLA Ops:
  7.2 0.0 copy-start
  7.2 0.0 all-gather.10.cloned.1.call-start
  7.2 1.2 fusion.1
  8.5 1.8 fusion.3
  10.3 0.0 all-gather.10.cloned.1.call-update
  10.3 1.2 dynamic-slice
  12.2 0.9 dynamic-update-slice
  13.1 13.1 %all-reduce = s32[512]{0:T(512)S(1)} all-reduce(s32[512]{0:T(512)S(1)} %dynamic-update-slice), channel_id=1, replica_groups=mesh['req'=8,'tp'=4] {'req'}, use_global_device_ids=true, to_apply=%add | all-reduce | flops 512 | bytes 4096
  26.2 36.2 %all-gather.10.cloned.1.call-done = bf16[512,2048]{1,0:T(8,128)(2,1)} async-done(((bf16[64,2048]{1,0:T(8,128)(2,1)}), bf16[512,2048]{1,0:T(8,128)(2,1)}) %all-gather.10.cloned.1.call-update) | async-done | bytes 2097168 | tf_op jit(solution)/shard_map/all_gather | solution.py:40
  62.4 0.0 copy-done
  62.4 2.6 %fusion.4 = (f32[512]{0:T(512)S(1)}, f32[512,384]{0,1:T(8,128)S(1)}) fusion(bf16[512,2048]{1,0:T(8,128)(2,1)} %all-gather.10.cloned.1.call-done, bf16[2048,384]{1,0:T(8,128)(2,1)S(1)} %copy-done), kind=kOutput, calls=%fused_computation.27 | convolution fusion | flops 805502464 | bytes 4458496 | tf_op jit(solution)/shard_map/dot_general | solution.py:39
  65.1 0.0 copy-start.1
  65.1 39.2 %all-gather.4 = f32[32,1,512]{2,1,0:T(1,128)S(1)} all-gather(f32[1,1,512]{2,1,0:T(1,128)S(1)} %bitcast.49), channel_id=2, replica_groups=mesh['req'=8,'tp'=4] {'req','tp'}, dimensions={0}, use_global_device_ids=true | all-gather | bytes 67584 | tf_op jit(solution)/shard_map/all_gather | solution.py:8
  104.3 0.3 multiply_reduce_fusion
  104.5 36.8 %all-gather.5 = f32[32,1,512]{2,1,0:T(1,128)S(1)} all-gather(f32[1,1,512]{2,1,0:T(1,128)S(1)} %bitcast.51), channel_id=3, replica_groups=mesh['req'=8,'tp'=4] {'req','tp'}, dimensions={0}, use_global_device_ids=true | all-gather | bytes 67584 | tf_op jit(solution)/shard_map/all_gather | solution.py:8
  141.3 38.1 %all-gather.6 = f32[32,1,512]{2,1,0:T(1,128)S(1)} all-gather(f32[1,1,512]{2,1,0:T(1,128)S(1)} %bitcast.50), channel_id=4, replica_groups=mesh['req'=8,'tp'=4] {'req','tp'}, dimensions={0}, use_global_device_ids=true | all-gather | bytes 67584 | tf_op jit(solution)/shard_map/all_gather | solution.py:8
  179.5 36.8 %all-gather.7 = f32[32,1,512]{2,1,0:T(1,128)S(1)} all-gather(f32[1,1,512]{2,1,0:T(1,128)S(1)} %bitcast.48), channel_id=5, replica_groups=mesh['req'=8,'tp'=4] {'req','tp'}, dimensions={0}, use_global_device_ids=true | all-gather | bytes 67584 | tf_op jit(solution)/shard_map/all_gather | solution.py:8
  216.4 3.6 %while.16 = (s32[]{:T(128)}, f32[512]{0:T(512)S(1)}, f32[512]{0:T(512)S(1)}, f32[512]{0:T(512)S(1)}, f32[512]{0:T(512)S(1)}, /*index=5*/f32[31,512]{1,0:T(8,128)...) while((s32[]{:T(128)}, f32[512]{0:T(512)S(1)}, f32[512]{0:T(512)S(1)}, ...), condition=%wide.region_6.7_spmd, body=%wide.region_5.6_spmd.sunk | while | flops 6146 | bytes 51317 | solution.py:11
  220.0 0.0 copy-done.1
  220.0 0.6 subtract_multiply_fusion
  (201 shorter events, 2.3 us)
Async XLA Ops:
  7.2 55.3 %copy-start = (bf16[2048,384]{1,0:T(8,128)(2,1)S(1)}, bf16[2048,384]{1,0:T(8,128)(2,1)}, u32[]{:S(2)}) copy-start(bf16[2048,384]{1,0:T(8,128)(2,1)} %param.9) | copy-start | bytes 4718596
  7.2 55.2 %all-gather.10.cloned.1.call-start = ((), (), s32[]{:S(2)}) async-start(), calls=%async_computation | async-start | bytes 2359296 | tf_op jit(solution)/shard_map/all_gather | solution.py:40
  65.1 154.9 %copy-start.1 = (s32[64]{0:T(128)S(1)}, s32[64]{0:T(128)}, u32[]{:S(2)}) copy-start(s32[64]{0:T(128)} %param.11) | copy-start | bytes 772
Sparse Core Ops, SparseCore 0:
  10.4 51.9 all-gather.9
where the time goes:
time: 228 us; the launch traced here: 227 us
  blocking collectives  164 us (72%)
  waiting for transfers between devices  36.3 us (16%)
  between operations  14.8 us (6%)
  other arithmetic  5.27 us (2%)
  local copies, waits for them, and re-layouts  3.05 us (1%)
  matrix products  2.63 us (1%)
    all_gather x4, blocking collectives, combined_all(): pieces = jax.tree.map(lambda part: lax.all_gather(part, axis), value)  151 us
    all_gather x1, waiting for transfers between devices, body(): lax.all_gather(normed, 'req', axis=0, tiled=True)  36.2 us
    unnamed x1, blocking collectives  13.1 us
  transfers between devices with their start and end apart: 1, of which 1 were waited for; matrix products, arithmetic and copies ran while one was open for 1% of the time, Pallas kernels for 0%

commit v1 on v0

--- a/solution.py
+++ b/solution.py
@@ -27,6 +27,30 @@
 
 
 def body(hidden, norm_gain, head_weight, targets, pad_mask):
+
+    def _note_rates(here_x):
+        y = lax.axis_size("req")
+        e_next = lax.axis_index("req")
+        r_now, built, far_arr = (y, e_next, here_x.shape[0])
+        items = [j0 * r_now if d == 0 else j0 for d, j0 in enumerate(here_x.shape)]
+        arr_out = current_value = here_x
+        left_arr = lax.dynamic_update_slice_in_dim(
+            jnp.zeros(items, here_x.dtype), here_x, built * far_arr, axis=0
+        )
+        for nth in range(1, r_now // 2 + 1):
+            arr_out = lax.ppermute(arr_out, "req", [(d, (d + 1) % r_now) for d in range(r_now)])
+            left_arr = lax.dynamic_update_slice_in_dim(
+                left_arr, arr_out, (built - nth) % r_now * far_arr, axis=0
+            )
+            if 2 * nth < r_now:
+                current_value = lax.ppermute(
+                    current_value, "req", [(d, (d - 1) % r_now) for d in range(r_now)]
+                )
+                left_arr = lax.dynamic_update_slice_in_dim(
+                    left_arr, current_value, (built + nth) % r_now * far_arr, axis=0
+                )
+        return left_arr
+
     slots = hidden.shape[0]
     voc_local = head_weight.shape[1]
     tp_count = lax.axis_size("tp")
@@ -36,11 +60,7 @@
     normed = (wide * scale * norm_gain[None, :]).astype(jnp.bfloat16)
     columns = lax.broadcasted_iota(jnp.int32, (1, voc_local), 1)
     all_targets = lax.all_gather(targets, "req", axis=0, tiled=True)
-    logits = jnp.dot(
-        lax.all_gather(normed, "req", axis=0, tiled=True),
-        head_weight,
-        preferred_element_type=jnp.float32,
-    )
+    logits = jnp.dot(_note_rates(normed), head_weight, preferred_element_type=jnp.float32)
     top_row = jnp.max(logits, axis=1)
     expo = jnp.exp(logits - top_row[:, None])
     local = all_targets - voc_start

time: 228 us -> 218 us (0.956)
  waiting for transfers between devices: 36.3 us -> 11.2 us
  starting transfers between devices: 0.04 us -> 20.5 us
  between operations: 14.8 us -> 1.44 us
  local copies, waits for them, and re-layouts: 3.05 us -> 8.42 us
  blocking collectives: 164 us -> 168 us
    all_gather x1 -> x0, waiting for transfers between devices: 36.2 us -> none  [body(): lax.all_gather(normed, 'req', axis=0, tiled=True)]
    ppermute x0 -> x7, starting transfers between devices: none -> 20.5 us  [the longest x3 12.6 us: _note_rates(): lax.ppermute(current_value, 'req', [(d, (d - 1) % r_now) for d in range(r...]
    ppermute x0 -> x7, waiting for transfers between devices: none -> 11.2 us  [the longest x3 7.42 us: _note_rates(): lax.ppermute(current_value, 'req', [(d, (d - 1) % r_now) for d in range(r...]
    dynamic_update_slice x0 -> x7, local copies, waits for them, and re-layouts: none -> 5.02 us  [the longest x4 2.9 us: _note_rates(): lax.dynamic_update_slice_in_dim(left_arr, arr_out, (built - nth) % r_now...]
    unnamed x1, blocking collectives: 13.1 us -> 16 us
  transfers between devices with their start and end apart: 1 -> 7, of which waited for: 1 -> 2; matrix products, arithmetic and copies ran while one was open for 1% -> 2% of each run, Pallas kernels for 0% -> 0%
where the time goes in v1:
time: 218 us; the launch traced here: 217 us
  blocking collectives  168 us (77%)
  starting transfers between devices  20.5 us (9%)
  waiting for transfers between devices  11.2 us (5%)
  local copies, waits for them, and re-layouts  8.42 us (4%)
  other arithmetic  4.29 us (2%)
  matrix products  2.63 us (1%)
    all_gather x4, blocking collectives, combined_all(): pieces = jax.tree.map(lambda part: lax.all_gather(part, axis), value)  152 us
    unnamed x1, blocking collectives  16 us
    ppermute x3, starting transfers between devices, _note_rates(): lax.ppermute(current_value, 'req', [(d, (d - 1) % r_now) for d in range(r...  12.6 us
    ppermute x4, starting transfers between devices, _note_rates(): lax.ppermute(arr_out, 'req', [(d, (d + 1) % r_now) for d in range(r_now)])  7.94 us
    ppermute x3, waiting for transfers between devices, _note_rates(): lax.ppermute(current_value, 'req', [(d, (d - 1) % r_now) for d in range(r...  7.42 us
  transfers between devices with their start and end apart: 7, of which 2 were waited for; matrix products, arithmetic and copies ran while one was open for 2% of the time, Pallas kernels for 0%

profile of v1, /device:TPU:0, one launch (start us, length us, event | category | flops | bytes accessed | tf_op | source)
XLA Modules:
  0.0 217.5 jit_solution(17901741085830032749)
XLA Ops:
  0.7 1.2 fusion.1
  1.9 1.6 broadcast_in_dim.5
  3.5 0.8 constant_dynamic-update-slice_fusion.7
  4.4 2.9 %collective-permute-start = (bf16[64,2048]{1,0:T(8,128)(2,1)S(1)}, bf16[64,2048]{1,0:T(8,128)(2,1)S(1)}, u32[]{:S(2)}, u32[]{:S(2)}) collective-permute-start(bf16[64,2048]{1,0:T(8,128)(2,1)S(1)} %get-tuple-element.80), channel_id=1, source_target_pairs={{0,4},{4,8},{8,12},{12,16},{16,20},{20,24},{24,28},{28,0},{1,5},{5... | collective-permute-start | bytes 786440 | tf_op jit(solution)/shard_map/ppermute | solution.py:41
  7.3 3.1 %collective-permute-start.1 = (bf16[64,2048]{1,0:T(8,128)(2,1)S(1)}, bf16[64,2048]{1,0:T(8,128)(2,1)S(1)}, u32[]{:S(2)}, u32[]{:S(2)}) collective-permute-start(bf16[64,2048]{1,0:T(8,128)(2,1)S(1)} %get-tuple-element.80), channel_id=1, source_target_pairs={{0,28},{4,0},{8,4},{12,8},{16,12},{20,16},{24,20},{28,24},{1,29},{... | collective-permute-start | bytes 786440 | tf_op jit(solution)/shard_map/ppermute | solution.py:46
  11.9 16.0 %all-reduce = s32[512]{0:T(512)S(1)} all-reduce(s32[512]{0:T(512)S(1)} %dynamic-update-slice), channel_id=1, replica_groups=mesh['req'=8,'tp'=4] {'req'}, use_global_device_ids=true, to_apply=%add | all-reduce | flops 512 | bytes 4096
  28.5 4.1 %collective-permute-start.3 = (bf16[64,2048]{1,0:T(8,128)(2,1)S(1)}, bf16[64,2048]{1,0:T(8,128)(2,1)S(1)}, u32[]{:S(2)}, u32[]{:S(2)}) collective-permute-start(bf16[64,2048]{1,0:T(8,128)(2,1)S(1)} %collective-permute-done.1), channel_id=1, source_target_pairs={{0,28},{4,0},{8,4},{12,8},{16,12},{20,16},{24,20},{28,24},{1,29},{... | collective-permute-start | bytes 786440 | tf_op jit(solution)/shard_map/ppermute | solution.py:46
  32.6 0.7 constant_dynamic-update-slice_fusion.6
  34.0 3.8 %collective-permute-done.2 = bf16[64,2048]{1,0:T(8,128)(2,1)S(1)} collective-permute-done((bf16[64,2048]{1,0:T(8,128)(2,1)S(1)}, bf16[64,2048]{1,0:T(8,128)(2,1)S(1)}, u32[]{:S(2)}, u32[]{:S(2)}) %collective-permute-start.2) | collective-permute-done | bytes 262176 | tf_op jit(solution)/shard_map/ppermute | solution.py:41
  37.8 2.5 %collective-permute-start.4 = (bf16[64,2048]{1,0:T(8,128)(2,1)S(1)}, bf16[64,2048]{1,0:T(8,128)(2,1)S(1)}, u32[]{:S(2)}, u32[]{:S(2)}) collective-permute-start(bf16[64,2048]{1,0:T(8,128)(2,1)S(1)} %collective-permute-done.2), channel_id=1, source_target_pairs={{0,4},{4,8},{8,12},{12,16},{16,20},{20,24},{24,28},{28,0},{1,5},{5... | collective-permute-start | bytes 786440 | tf_op jit(solution)/shard_map/ppermute | solution.py:41
  40.3 5.4 %collective-permute-start.5 = (bf16[64,2048]{1,0:T(8,128)(2,1)S(1)}, bf16[64,2048]{1,0:T(8,128)(2,1)S(1)}, u32[]{:S(2)}, u32[]{:S(2)}) collective-permute-start(bf16[64,2048]{1,0:T(8,128)(2,1)S(1)} %collective-permute-done.3), channel_id=1, source_target_pairs={{0,28},{4,0},{8,4},{12,8},{16,12},{20,16},{24,20},{28,24},{1,29},{... | collective-permute-start | bytes 786440 | tf_op jit(solution)/shard_map/ppermute | solution.py:46
  45.7 0.7 constant_dynamic-update-slice_fusion.4
  46.4 0.7 constant_dynamic-update-slice_fusion.3
  47.1 1.9 collective-permute-start.6
  49.0 0.7 constant_dynamic-update-slice_fusion.2
  49.7 7.4 %collective-permute-done.5 = bf16[64,2048]{1,0:T(8,128)(2,1)S(1)} collective-permute-done((bf16[64,2048]{1,0:T(8,128)(2,1)S(1)}, bf16[64,2048]{1,0:T(8,128)(2,1)S(1)}, u32[]{:S(2)}, u32[]{:S(2)}) %collective-permute-start.5) | collective-permute-done | bytes 262176 | tf_op jit(solution)/shard_map/ppermute | solution.py:46
  57.1 0.7 constant_dynamic-update-slice_fusion.1
  57.8 0.7 constant_dynamic-update-slice_fusion
  58.6 2.6 %fusion.5 = (f32[512]{0:T(512)S(1)}, f32[512,384]{0,1:T(8,128)S(1)}) fusion(bf16[512,2048]{1,0:T(8,128)(2,1)} %constant_dynamic-update-slice_fusion, bf16[2048,384]{1,0:T(8,128)(2,1)S(1)} %copy-done), kind=kOutput, calls=%fused_computation.35 | convolution fusion | flops 805502464 | bytes 4458496 | tf_op jit(solution)/shard_map/dot_general | solution.py:63
  61.5 39.9 %all-gather.7 = f32[32,1,512]{2,1,0:T(1,128)S(1)} all-gather(f32[1,1,512]{2,1,0:T(1,128)S(1)} %bitcast.51), channel_id=5, replica_groups=mesh['req'=8,'tp'=4] {'req','tp'}, dimensions={0}, use_global_device_ids=true | all-gather | bytes 67584 | tf_op jit(solution)/shard_map/all_gather | solution.py:8
  101.4 36.8 %all-gather.5 = f32[32,1,512]{2,1,0:T(1,128)S(1)} all-gather(f32[1,1,512]{2,1,0:T(1,128)S(1)} %bitcast.50), channel_id=3, replica_groups=mesh['req'=8,'tp'=4] {'req','tp'}, dimensions={0}, use_global_device_ids=true | all-gather | bytes 67584 | tf_op jit(solution)/shard_map/all_gather | solution.py:8
  138.2 38.1 %all-gather.6 = f32[32,1,512]{2,1,0:T(1,128)S(1)} all-gather(f32[1,1,512]{2,1,0:T(1,128)S(1)} %bitcast.49), channel_id=4, replica_groups=mesh['req'=8,'tp'=4] {'req','tp'}, dimensions={0}, use_global_device_ids=true | all-gather | bytes 67584 | tf_op jit(solution)/shard_map/all_gather | solution.py:8
  176.3 36.8 %all-gather.4 = f32[32,1,512]{2,1,0:T(1,128)S(1)} all-gather(f32[1,1,512]{2,1,0:T(1,128)S(1)} %bitcast.48), channel_id=2, replica_groups=mesh['req'=8,'tp'=4] {'req','tp'}, dimensions={0}, use_global_device_ids=true | all-gather | bytes 67584 | tf_op jit(solution)/shard_map/all_gather | solution.py:8
  213.2 3.6 %while.16 = (s32[]{:T(128)}, f32[512]{0:T(512)S(1)}, f32[512]{0:T(512)S(1)}, f32[512]{0:T(512)S(1)}, f32[512]{0:T(512)S(1)}, /*index=5*/f32[31,512]{1,0:T(8,128)...) while((s32[]{:T(128)}, f32[512]{0:T(512)S(1)}, f32[512]{0:T(512)S(1)}, ...), condition=%wide.region_6.7_spmd, body=%wide.region_5.6_spmd.sunk | while | flops 6146 | bytes 51309 | solution.py:11
  (224 shorter events, 5.4 us)
Async XLA Ops:
  0.6 57.9 %copy-start = (bf16[2048,384]{1,0:T(8,128)(2,1)S(1)}, bf16[2048,384]{1,0:T(8,128)(2,1)}, u32[]{:S(2)}) copy-start(bf16[2048,384]{1,0:T(8,128)(2,1)} %param.9) | copy-start | bytes 4718596
  0.6 9.7 %copy-start.5 = (u32[32]{0:T(128)S(1)}, u32[32]{0:T(128)}, u32[]{:S(2)}) copy-start(u32[32]{0:T(128)} %constant.92) | copy-start | bytes 388
  0.7 2.9 %copy-start.1 = (bf16[64,2048]{1,0:T(8,128)(2,1)S(1)}, bf16[64,2048]{1,0:T(8,128)(2,1)}, u32[]{:S(2)}) copy-start(bf16[64,2048]{1,0:T(8,128)(2,1)} %param.7) | copy-start | bytes 786436
  0.7 2.9 %copy-start.2 = (f32[2048]{0:T(1024)S(1)}, f32[2048]{0:T(1024)}, u32[]{:S(2)}) copy-start(f32[2048]{0:T(1024)} %param.8) | copy-start | bytes 24580
  0.7 10.9 %copy-start.4 = (s32[64]{0:T(128)S(1)}, s32[64]{0:T(128)}, u32[]{:S(2)}) copy-start(s32[64]{0:T(128)} %param.10) | copy-start | bytes 772
  4.4 23.5 %collective-permute-start = (bf16[64,2048]{1,0:T(8,128)(2,1)S(1)}, bf16[64,2048]{1,0:T(8,128)(2,1)S(1)}, u32[]{:S(2)}, u32[]{:S(2)}) collective-permute-start(bf16[64,2048]{1,0:T(8,128)(2,1)S(1)} %get-tuple-element.80), channel_id=1, source_target_pairs={{0,4},{4,8},{8,12},{12,16},{16,20},{20,24},{24,28},{28,0},{1,5},{5... | collective-permute-start | bytes 786440 | tf_op jit(solution)/shard_map/ppermute | solution.py:41
  7.3 21.2 %collective-permute-start.1 = (bf16[64,2048]{1,0:T(8,128)(2,1)S(1)}, bf16[64,2048]{1,0:T(8,128)(2,1)S(1)}, u32[]{:S(2)}, u32[]{:S(2)}) collective-permute-start(bf16[64,2048]{1,0:T(8,128)(2,1)S(1)} %get-tuple-element.80), channel_id=1, source_target_pairs={{0,28},{4,0},{8,4},{12,8},{16,12},{20,16},{24,20},{28,24},{1,29},{... | collective-permute-start | bytes 786440 | tf_op jit(solution)/shard_map/ppermute | solution.py:46
  27.8 10.0 %collective-permute-start.2 = (bf16[64,2048]{1,0:T(8,128)(2,1)S(1)}, bf16[64,2048]{1,0:T(8,128)(2,1)S(1)}, u32[]{:S(2)}, u32[]{:S(2)}) collective-permute-start(bf16[64,2048]{1,0:T(8,128)(2,1)S(1)} %collective-permute-done), channel_id=1, source_target_pairs={{0,4},{4,8},{8,12},{12,16},{16,20},{20,24},{24,28},{28,0},{1,5},{5... | collective-permute-start | bytes 786440 | tf_op jit(solution)/shard_map/ppermute | solution.py:41
  28.5 11.8 %collective-permute-start.3 = (bf16[64,2048]{1,0:T(8,128)(2,1)S(1)}, bf16[64,2048]{1,0:T(8,128)(2,1)S(1)}, u32[]{:S(2)}, u32[]{:S(2)}) collective-permute-start(bf16[64,2048]{1,0:T(8,128)(2,1)S(1)} %collective-permute-done.1), channel_id=1, source_target_pairs={{0,28},{4,0},{8,4},{12,8},{16,12},{20,16},{24,20},{28,24},{1,29},{... | collective-permute-start | bytes 786440 | tf_op jit(solution)/shard_map/ppermute | solution.py:46
  37.8 9.3 %collective-permute-start.4 = (bf16[64,2048]{1,0:T(8,128)(2,1)S(1)}, bf16[64,2048]{1,0:T(8,128)(2,1)S(1)}, u32[]{:S(2)}, u32[]{:S(2)}) collective-permute-start(bf16[64,2048]{1,0:T(8,128)(2,1)S(1)} %collective-permute-done.2), channel_id=1, source_target_pairs={{0,4},{4,8},{8,12},{12,16},{16,20},{20,24},{24,28},{28,0},{1,5},{5... | collective-permute-start | bytes 786440 | tf_op jit(solution)/shard_map/ppermute | solution.py:41
  40.3 16.8 %collective-permute-start.5 = (bf16[64,2048]{1,0:T(8,128)(2,1)S(1)}, bf16[64,2048]{1,0:T(8,128)(2,1)S(1)}, u32[]{:S(2)}, u32[]{:S(2)}) collective-permute-start(bf16[64,2048]{1,0:T(8,128)(2,1)S(1)} %collective-permute-done.3), channel_id=1, source_target_pairs={{0,28},{4,0},{8,4},{12,8},{16,12},{20,16},{24,20},{28,24},{1,29},{... | collective-permute-start | bytes 786440 | tf_op jit(solution)/shard_map/ppermute | solution.py:46
  47.1 10.7 %collective-permute-start.6 = (bf16[64,2048]{1,0:T(8,128)(2,1)S(1)}, bf16[64,2048]{1,0:T(8,128)(2,1)S(1)}, u32[]{:S(2)}, u32[]{:S(2)}) collective-permute-start(bf16[64,2048]{1,0:T(8,128)(2,1)S(1)} %collective-permute-done.4), channel_id=1, source_target_pairs={{0,4},{4,8},{8,12},{12,16},{16,20},{20,24},{24,28},{28,0},{1,5},{5... | collective-permute-start | bytes 786440 | tf_op jit(solution)/shard_map/ppermute | solution.py:41
  61.2 155.7 %copy-start.3 = (s32[64]{0:T(128)S(1)}, s32[64]{0:T(128)}, u32[]{:S(2)}) copy-start(s32[64]{0:T(128)} %param.11) | copy-start | bytes 772
